TPU v7x, 32 devices: a whole 2x2x4 slice. The times are simulated.
32 devices in a mesh: dp: 8 (over y, x, core), fsdp: 4 (over z).
Axes of the slice: x: 2, y: 2, z: 4, core: 2. Of those that a mesh axis runs over, the one named last changes fastest.
Arguments:
- tokens: bfloat16 [1024, 5120], P('dp'), may hold values from -6 to 6
- targets: bfloat16 [1024, 5120], P('dp'), may hold values from -12 to 12
- norm_gain: float32 [5120], replicated, may hold values from 0.5 to 1.5
- up_master: float32 [5120, 6912], P('dp', 'fsdp'), may hold values from -0.078125 to 0.078125
- down_master: float32 [6912, 5120], P('fsdp', 'dp'), may hold values from -0.078125 to 0.078125
- up_probe: int32 [160, 6912], P(None, 'fsdp'), may hold values from -2147483648 to 2147483646
- down_probe: int32 [6912, 160], P('fsdp'), may hold values from -2147483648 to 2147483646
- up_first: float32 [5120, 6912], P('dp', 'fsdp'), may hold values from -0.012 to 0.012
- up_second: float32 [5120, 6912], P('dp', 'fsdp'), may hold values from 0.0001 to 0.001
- down_first: float32 [6912, 5120], P('fsdp', 'dp'), may hold values from -0.012 to 0.012
- down_second: float32 [6912, 5120], P('fsdp', 'dp'), may hold values from 0.0001 to 0.001
Outputs:
- loss: float32 [], replicated
- up_moment: float32 [5120, 6912], P('dp', 'fsdp')
- up_curvature: float32 [5120, 6912], P('dp', 'fsdp')
- up_step: float32 [5120, 6912], P('dp', 'fsdp')
- down_moment: float32 [6912, 5120], P('fsdp', 'dp')
- down_curvature: float32 [6912, 5120], P('fsdp', 'dp')
- down_step: float32 [6912, 5120], P('fsdp', 'dp')
Inputs may be any that keep to these rules, and one draw needn't show every extreme that they name: `up_probe`: any 32-bit word; each bit gives one probe sign. `down_probe`: any 32-bit word; each bit gives one probe sign.
All inputs are finite; a program needn't handle non-finite values.
Results may differ from a plain program's by a relative error of at most 0.03.
Values may be sent and summed in bfloat16 or wider, within the bound.
A program may use at most 320 MiB of HBM per device.

v0:
```python
import jax
import jax.numpy as jnp
from jax import lax
from jax.sharding import PartitionSpec as P

BLOCK = 16
STEP = 10


norm_eps = 1e-05
beta_one = 0.9
beta_two = 0.999
adam_eps = 1e-08


def signs_rows(probe):
    shifts = jnp.arange(32, dtype=jnp.int32)[:, None, None]
    bits = jnp.bitwise_and(jnp.right_shift(probe[None, :, :], shifts), 1)
    return (1 - 2 * bits).reshape(32 * probe.shape[0], probe.shape[1]).astype(jnp.bfloat16)


def signs_cols(probe):
    shifts = jnp.arange(32, dtype=jnp.int32)[None, :, None]
    bits = jnp.bitwise_and(jnp.right_shift(probe[:, None, :], shifts), 1)
    return (1 - 2 * bits).reshape(probe.shape[0], 32 * probe.shape[1]).astype(jnp.bfloat16)


def dot_last(left, right):
    return lax.dot_general(
        left, right, (((1,), (1,)), ((), ())), preferred_element_type=jnp.float32
    )


def rounded(value):
    return lax.optimization_barrier(value.astype(jnp.bfloat16)).astype(jnp.float32)


def moments(grad, hess, signs, first, second):
    hut = jnp.abs(signs * hess)
    rows, cols = hut.shape
    means = jnp.mean(hut.reshape(rows, cols // BLOCK, BLOCK), axis=-1)
    diag = jnp.repeat(means, BLOCK, axis=1)
    first_new = beta_one * first + (1.0 - beta_one) * grad
    second_new = beta_two * second + (1.0 - beta_two) * diag * diag
    direction = (
        first_new
        / (1.0 - beta_one**STEP)
        / (jnp.sqrt(second_new / (1.0 - beta_two**STEP)) + adam_eps)
    )
    return (first_new, second_new, direction)


def local(
    tokens,
    targets,
    norm_gain,
    up_master,
    down_master,
    up_probe,
    down_probe,
    up_first,
    up_second,
    down_first,
    down_second,
):
    tok_rows = tokens.shape[0]
    tokens_all = jnp.float32(tok_rows * lax.axis_size("dp"))
    up_signs = signs_rows(up_probe)
    down_signs = signs_cols(down_probe)
    up_full, down_full = (
        lax.all_gather(up_master.astype(jnp.bfloat16), "dp", axis=0, tiled=True),
        lax.all_gather(down_master.astype(jnp.bfloat16), "dp", axis=1, tiled=True),
    )
    values = tokens.astype(jnp.float32)
    scale = lax.rsqrt(jnp.mean(values * values, axis=-1, keepdims=True) + norm_eps)
    normed = (values * scale * norm_gain).astype(jnp.bfloat16)
    preact = jnp.dot(normed, up_full, preferred_element_type=jnp.float32)
    logistic = jax.nn.sigmoid(preact)
    active = (preact * logistic).astype(jnp.bfloat16)
    slopes = logistic * (1.0 + preact * (1.0 - logistic))
    curves = logistic * (1.0 - logistic) * (2.0 + preact * (1.0 - 2.0 * logistic))
    preact_dir = jnp.dot(normed, up_signs, preferred_element_type=jnp.float32)
    active_dir = (slopes * preact_dir).astype(jnp.bfloat16)
    partial_value = jnp.dot(active, down_full, preferred_element_type=jnp.float32)
    partial_dir = jnp.dot(active_dir, down_full, preferred_element_type=jnp.float32) + jnp.dot(
        active, down_signs, preferred_element_type=jnp.float32
    )
    output, output_dir = (
        lax.psum(partial_value.astype(jnp.bfloat16), "fsdp").astype(jnp.float32),
        lax.psum(partial_dir.astype(jnp.bfloat16), "fsdp").astype(jnp.float32),
    )
    diff = output - targets.astype(jnp.float32)
    residual = (diff / tokens_all).astype(jnp.bfloat16)
    residual_dir = (output_dir / tokens_all).astype(jnp.bfloat16)
    loss = lax.psum(0.5 * jnp.sum(diff * diff) / tokens_all, "dp")
    grad_active = dot_last(residual, down_full)
    hess_active = dot_last(residual_dir, down_full) + dot_last(residual, down_signs)
    grad_preact = (slopes * grad_active).astype(jnp.bfloat16)
    hess_preact = (curves * preact_dir * grad_active + slopes * hess_active).astype(jnp.bfloat16)
    own_rows = up_master.shape[0]
    hidden = up_master.shape[1]
    offset = lax.axis_index("dp") * own_rows
    owned_in, owned_res, owned_dir = (
        lax.all_to_all(normed, "dp", split_axis=1, concat_axis=0, tiled=True),
        lax.all_to_all(residual, "dp", split_axis=1, concat_axis=0, tiled=True),
        lax.all_to_all(residual_dir, "dp", split_axis=1, concat_axis=0, tiled=True),
    )
    piece_grad = lax.all_gather(grad_preact, "dp", axis=0, tiled=True)
    piece_hess = lax.all_gather(hess_preact, "dp", axis=0, tiled=True)
    piece_act = lax.all_gather(active, "dp", axis=0, tiled=True)
    piece_actdir = lax.all_gather(active_dir, "dp", axis=0, tiled=True)
    count = piece_grad.shape[0]
    blocks = count // tok_rows
    inputs = owned_in.reshape(blocks, tok_rows, own_rows)
    resids = owned_res.reshape(blocks, tok_rows, own_rows)
    resdirs = owned_dir.reshape(blocks, tok_rows, own_rows)
    grads3 = piece_grad.reshape(blocks, tok_rows, hidden)
    hess3 = piece_hess.reshape(blocks, tok_rows, hidden)
    act3 = piece_act.reshape(blocks, tok_rows, hidden)
    actdir3 = piece_actdir.reshape(blocks, tok_rows, hidden)
    up_g = jnp.einsum("btd,btf->bdf", inputs, grads3, preferred_element_type=jnp.float32)
    up_h = jnp.einsum("btd,btf->bdf", inputs, hess3, preferred_element_type=jnp.float32)
    down_g = jnp.einsum("btf,btd->bfd", act3, resids, preferred_element_type=jnp.float32)
    down_h = jnp.einsum(
        "btf,btd->bfd", act3, resdirs, preferred_element_type=jnp.float32
    ) + jnp.einsum("btf,btd->bfd", actdir3, resids, preferred_element_type=jnp.float32)
    up_grad = jnp.sum(rounded(up_g), axis=0)
    up_hess = jnp.sum(rounded(up_h), axis=0)
    down_grad = jnp.sum(rounded(down_g), axis=0)
    down_hess = jnp.sum(rounded(down_h), axis=0)
    up_own = lax.dynamic_slice_in_dim(up_signs, offset, own_rows, 0).astype(jnp.float32)
    down_own = lax.dynamic_slice_in_dim(down_signs, offset, own_rows, 1).astype(jnp.float32)
    up_moment, up_curvature, up_step = moments(up_grad, up_hess, up_own, up_first, up_second)
    down_moment, down_curvature, down_step = moments(
        down_grad, down_hess, down_own, down_first, down_second
    )
    return (loss, up_moment, up_curvature, up_step, down_moment, down_curvature, down_step)


def solution(mesh):
    placed = (
        P("dp", None),
        P("dp", None),
        P(),
        P("dp", "fsdp"),
        P("fsdp", "dp"),
        P(None, "fsdp"),
        P("fsdp", None),
        P("dp", "fsdp"),
        P("dp", "fsdp"),
        P("fsdp", "dp"),
        P("fsdp", "dp"),
    )
    return jax.shard_map(
        local,
        mesh=mesh,
        in_specs=placed,
        out_specs=(
            P(),
            P("dp", "fsdp"),
            P("dp", "fsdp"),
            P("dp", "fsdp"),
            P("fsdp", "dp"),
            P("fsdp", "dp"),
            P("fsdp", "dp"),
        ),
        check_vma=False,
    )
```

profile of v0, /device:TPU:1, one launch (start us, length us, event | category | flops | bytes accessed | tf_op | source)
XLA Modules:
  0.0 565.4 jit_solution(4920918332310824843)
XLA Ops:
  15.9 14.9 %shift_right_arithmetic.40 = s32[32,160,1728]{2,1,0:T(8,128)} broadcast(s32[160,1728]{1,0:T(8,128)} %param.16), dimensions={1,2} | broadcast | bytes 36495360 | tf_op jit(solution)/shard_map/shift_right_arithmetic | solution.py:18
  30.8 37.1 %copy.59 = s32[5120,1728]{0,1:T(8,128)} copy(s32[5120,1728]{1,0:T(8,128)} %bitcast.85) | data formatting | bytes 70778880 | tf_op jit(solution)/shard_map/shift_right_arithmetic | solution.py:18
  68.1 12.3 %shift_right_arithmetic.46 = s32[1728,32,160]{0,2,1:T(8,128)} broadcast(s32[1728,160]{0,1:T(8,128)S(1)} %copy-done.14), dimensions={0,2} | broadcast | bytes 36495360 | tf_op jit(solution)/shard_map/shift_right_arithmetic | solution.py:24
  80.4 36.8 %copy.60 = s32[1728,5120]{1,0:T(8,128)} copy(s32[1728,5120]{0,1:T(8,128)} %bitcast.86) | data formatting | bytes 70778880 | tf_op jit(solution)/shard_map/shift_right_arithmetic | solution.py:24
  120.2 23.3 %subtract_convert_fusion.1 = bf16[5120,1728]{0,1:T(8,128)(2,1)} fusion(s32[5120,1728]{0,1:T(8,128)} %copy.59, s32[5120]{0:T(1024)S(1)} %shift_right_arithmetic.43), kind=kLoop, calls=%fused_computation.5 | loop fusion | flops 44236800 | bytes 53104640 | tf_op jit(solution)/shard_map/convert_element_type | solution.py:19
  148.4 10.5 %subtract_convert_fusion = bf16[1728,5120]{1,0:T(8,128)(2,1)} fusion(s32[1728,5120]{1,0:T(8,128)S(1)} %copy-done.1, s32[5120]{0:T(1024)S(1)} %shift_right_arithmetic.43), kind=kLoop, calls=%fused_computation.4 | loop fusion | flops 44236800 | bytes 53104640 | tf_op jit(solution)/shard_map/convert_element_type | solution.py:25
  158.9 9.0 %fusion.34 = f32[128,1728]{0,1:T(8,128)S(1)} fusion(bf16[5120,1728]{0,1:T(8,128)(2,1)} %all-gather.7.cloned.1.call-done, bf16[128,5120]{0,1:T(8,128)(2,1)S(1)} %fusion.16), kind=kOutput, calls=%fused_computation.71 | convolution fusion | flops 2264924160 | bytes 19890176 | tf_op jit(solution)/shard_map/dot_general | solution.py:77
  176.5 26.4 %all-gather.9.cloned.1.call-done = bf16[1728,5120]{1,0:T(8,128)(2,1)} async-done(((bf16[1728,640]{1,0:T(8,128)(2,1)}), bf16[1728,5120]{1,0:T(8,128)(2,1)}) %all-gather.9.cloned.1.call-update) | async-done | bytes 17694736 | tf_op jit(solution)/shard_map/all_gather | solution.py:72
  203.0 8.6 %fusion.33 = f32[128,5120]{1,0:T(8,128)S(1)} fusion(bf16[128,1728]{0,1:T(8,128)(2,1)S(1)} %get-tuple-element.31, bf16[1728,5120]{1,0:T(8,128)(2,1)} %all-gather.9.cloned.1.call-done), kind=kOutput, calls=%fused_computation.70 | convolution fusion | flops 2264924160 | bytes 20758528 | tf_op jit(solution)/shard_map/dot_general | solution.py:85
  211.6 9.9 %fusion = bf16[128,5120]{1,0:T(8,128)(2,1)} fusion(f32[128,5120]{1,0:T(8,128)S(1)} %fusion.33, bf16[128,1728]{0,1:T(8,128)(2,1)S(1)} %get-tuple-element.32, bf16[1728,5120]{1,0:T(8,128)(2,1)} %subtract_convert_fusion), kind=kOutput, calls=%fused_computation.15 | convolution fusion | flops 2266234880 | bytes 22069248 | tf_op jit(solution)/shard_map/dot_general | solution.py:85
  228.5 102.5 %all-reduce.3.cloned.1.call-done = (bf16[128,5120]{1,0:T(8,128)(2,1)}, bf16[128,5120]{1,0:T(8,128)(2,1)}) async-done(((bf16[128,5120]{1,0:T(8,128)(2,1)}, bf16[128,5120]{1,0:T(8,128)(2,1)}), (bf16[128,5120]{1,0:T(8,128)(2,1)}, bf16[128,5120]{1,0:T(8,128)(2,1)})) %all-reduce.3.cloned.1.call-update) | async-done | bytes 2621456 | tf_op jit(solution)/shard_map/psum | solution.py:89
  334.1 9.3 %fusion.30 = f32[128,1728]{0,1:T(8,128)S(1)} fusion(bf16[1728,5120]{1,0:T(8,128)(2,1)} %all-gather.9.cloned.1.call-done, bf16[128,5120]{1,0:T(8,128)(2,1)S(1)} %copy-done.6), kind=kOutput, calls=%fused_computation.69 | convolution fusion | flops 2266890240 | bytes 19890176 | tf_op jit(solution)/shard_map/dot_general | solution.py:29
  350.7 10.7 %fusion.19 = bf16[128,1728]{0,1:T(8,128)(2,1)} fusion(f32[128,1728]{0,1:T(8,128)S(1)} %fusion.30, bf16[128,5120]{1,0:T(8,128)(2,1)S(1)} %get-tuple-element.29, bf16[1728,5120]{1,0:T(8,128)(2,1)} %subtract_convert_fusion, f32[128,1728]{0,1:T(8,128)S(1)} %get-tuple-element.35, f32[128,1728]{0,1:T(8,128)} %get-tuple-element.33, f32[128,1728]{0,1:T(8,128)S(1)} %copy-done.17), kind=kOutput, calls=%fused_computation.47 | convolution fusion | flops 2269126656 | bytes 22986752 | tf_op jit(solution)/shard_map/dot_general | solution.py:29
  370.4 25.8 %psum.22 = f32[]{:T(128)} all-reduce(f32[]{:T(128)S(6)} %div.63), channel_id=1, replica_groups=mesh['dp'=8,'fsdp'=4] {'dp'}, use_global_device_ids=true, to_apply=%region_3.0 | all-reduce | flops 1 | bytes 8 | tf_op jit(solution)/shard_map/psum | solution.py:95
  402.2 15.4 %fusion.5 = f32[8,1728,640]{2,1,0:T(8,128)} fusion(bf16[128,8,640]{2,0,1:T(8,128)(2,1)S(1)} %all-to-all-done.2, bf16[1024,1728]{0,1:T(8,128)(2,1)} %all-gather.15.cloned.1.call-done), kind=kOutput, calls=%fused_computation.26 | convolution fusion | flops 2264924160 | bytes 40239104 | tf_op jit(solution)/shard_map/btf,btd->bfd/dot_general | solution.py:124
  424.8 21.0 %add_convert_fusion = bf16[8,1728,640]{2,1,0:T(8,128)(2,1)} fusion(f32[8,1728,640]{2,1,0:T(8,128)} %fusion.5, bf16[128,8,640]{2,0,1:T(8,128)(2,1)S(1)} %all-to-all-done.1, bf16[1024,1728]{0,1:T(8,128)(2,1)} %all-gather.17.cloned.1.call-done), kind=kOutput, calls=%fused_computation.1 | convolution fusion | flops 2282618880 | bytes 57933824 | tf_op jit(solution)/shard_map/btf,btd->bfd/dot_general | solution.py:126
  445.8 7.2 %convert_reduce_fusion = f32[1728,640]{1,0:T(8,128)S(1)} fusion(bf16[8,1728,640]{2,1,0:T(8,128)(2,1)} %add_convert_fusion), kind=kLoop, calls=%fused_computation | loop fusion | flops 16588800 | bytes 22118400 | tf_op jit(solution)/shard_map/reduce_sum | solution.py:130
  467.4 9.8 %convolution_convert_fusion.2 = bf16[8,1728,640]{2,1,0:T(8,128)(2,1)} fusion(bf16[128,8,640]{2,0,1:T(8,128)(2,1)} %copy-done.5, bf16[1024,1728]{0,1:T(8,128)(2,1)S(1)} %copy-done.3), kind=kOutput, calls=%fused_computation.9 | convolution fusion | flops 2273771520 | bytes 22544384 | tf_op jit(solution)/shard_map/btf,btd->bfd/dot_general | solution.py:123
  485.5 9.4 %convert_reduce_fusion.1 = f32[1728,640]{1,0:T(8,128)S(1)} fusion(bf16[8,1728,640]{2,1,0:T(8,128)(2,1)} %convolution_convert_fusion.2), kind=kLoop, calls=%fused_computation.2 | loop fusion | flops 16588800 | bytes 22118400 | tf_op jit(solution)/shard_map/reduce_sum | solution.py:129
  502.1 10.3 %convolution_convert_fusion = bf16[8,640,1728]{1,2,0:T(8,128)(2,1)} fusion(bf16[128,8,640]{2,0,1:T(8,128)(2,1)} %all-to-all-done, bf16[1024,1728]{0,1:T(8,128)(2,1)} %all-gather.13.cloned.1.call-done), kind=kOutput, calls=%fused_computation.7 | convolution fusion | flops 2273771520 | bytes 22544384 | tf_op jit(solution)/shard_map/btd,btf->bdf/dot_general | solution.py:122
  512.4 7.4 %convert_reduce_fusion.2 = f32[640,1728]{0,1:T(8,128)S(1)} fusion(bf16[8,640,1728]{1,2,0:T(8,128)(2,1)} %convolution_convert_fusion), kind=kLoop, calls=%fused_computation.3 | loop fusion | flops 16588800 | bytes 22118400 | tf_op jit(solution)/shard_map/reduce_sum | solution.py:128
  527.2 10.4 %convolution_convert_fusion.1 = bf16[8,640,1728]{1,2,0:T(8,128)(2,1)} fusion(bf16[128,8,640]{2,0,1:T(8,128)(2,1)} %all-to-all-done, bf16[1024,1728]{0,1:T(8,128)(2,1)} %all-gather.11.cloned.1.call-done), kind=kOutput, calls=%fused_computation.8 | convolution fusion | flops 2273771520 | bytes 22544384 | tf_op jit(solution)/shard_map/btd,btf->bdf/dot_general | solution.py:121
  537.7 9.3 %convert_reduce_fusion.3 = f32[640,1728]{0,1:T(8,128)} fusion(bf16[8,640,1728]{1,2,0:T(8,128)(2,1)} %convolution_convert_fusion.1), kind=kLoop, calls=%fused_computation.6 | loop fusion | flops 16588800 | bytes 22118400 | tf_op jit(solution)/shard_map/reduce_sum | solution.py:127
  547.0 11.3 %add_divide_fusion.1 = (f32[640,1728]{0,1:T(8,128)}, f32[640,1728]{0,1:T(8,128)}, f32[640,1728]{0,1:T(8,128)}) fusion(f32[640,108]{0,1:T(8,128)S(1)} %broadcast_multiply_fusion.1, f32[640,1728]{0,1:T(8,128)} %param.19, f32[640,1728]{0,1:T(8,128)} %convert_reduce_fusion.3, f32[640,1728]{0,1:T(8,128)} %param.18), kind=kLoop, calls=%fused_computation.21 | loop fusion | flops 12165120 | bytes 26818560 | tf_op jit(solution)/shard_map/div | solution.py:46
  (103 shorter events, 101.2 us)
Async XLA Ops:
  7.2 151.7 %all-gather.7.cloned.1.call-start = ((), (), s32[]{:S(2)}) async-start(), calls=%async_computation.3 | async-start | bytes 19906560 | tf_op jit(solution)/shard_map/all_gather | solution.py:71
  11.1 191.9 %all-gather.9.cloned.1.call-start = ((), (), s32[]{:S(2)}) async-start(), calls=%async_computation.4 | async-start | bytes 19906560 | tf_op jit(solution)/shard_map/all_gather | solution.py:72
  15.1 315.8 %all-reduce.3.cloned.1.call-start = ((), (), s32[]{:S(2)}) async-start(), calls=%async_computation.9 | async-start | bytes 5242880 | tf_op jit(solution)/shard_map/psum | solution.py:89
  30.8 37.2 %copy-start.14 = (s32[1728,160]{0,1:T(8,128)S(1)}, s32[1728,160]{0,1:T(8,128)}, u32[]{:S(2)}) copy-start(s32[1728,160]{0,1:T(8,128)} %param.17) | copy-start | bytes 3317764
  80.4 37.5 %copy-start.15 = (f32[5120]{0:T(1024)S(1)}, f32[5120]{0:T(1024)}, u32[]{:S(2)}) copy-start(f32[5120]{0:T(1024)} %param.13) | copy-start | bytes 61444
  120.1 47.7 %copy-start.7 = (bf16[128,5120]{0,1:T(8,128)(2,1)}, bf16[128,5120]{0,1:T(8,128)(2,1)S(1)}, u32[]{:S(2)}) copy-start(bf16[128,5120]{0,1:T(8,128)(2,1)S(1)} %fusion.16) | copy-start | bytes 3932164
  120.2 28.3 %copy-start.1 = (s32[1728,5120]{1,0:T(8,128)S(1)}, s32[1728,5120]{1,0:T(8,128)}, u32[]{:S(2)}) copy-start(s32[1728,5120]{1,0:T(8,128)} %copy.60) | copy-start | bytes 106168320
  158.9 11.5 %copy-start.2 = (bf16[5120,1728]{0,1:T(8,128)(2,1)S(1)}, bf16[5120,1728]{0,1:T(8,128)(2,1)}, u32[]{:S(2)}) copy-start(bf16[5120,1728]{0,1:T(8,128)(2,1)} %subtract_convert_fusion.1) | copy-start | bytes 53084164
  176.5 35.1 %copy-start.11 = (bf16[128,1728]{0,1:T(8,128)(2,1)}, bf16[128,1728]{0,1:T(8,128)(2,1)S(1)}, u32[]{:S(2)}) copy-start(bf16[128,1728]{0,1:T(8,128)(2,1)S(1)} %get-tuple-element.31) | copy-start | bytes 1327108
  176.5 45.0 %copy-start.10 = (bf16[128,1728]{0,1:T(8,128)(2,1)}, bf16[128,1728]{0,1:T(8,128)(2,1)S(1)}, u32[]{:S(2)}) copy-start(bf16[128,1728]{0,1:T(8,128)(2,1)S(1)} %get-tuple-element.32) | copy-start | bytes 1327108
  211.6 11.5 %copy-start = (bf16[1728,5120]{1,0:T(8,128)(2,1)S(1)}, bf16[1728,5120]{1,0:T(8,128)(2,1)}, u32[]{:S(2)}) copy-start(bf16[1728,5120]{1,0:T(8,128)(2,1)} %all-gather.9.cloned.1.call-done) | copy-start | bytes 53084164
  227.2 116.2 %slice-start = ((s8[17694720]{0:T(1024)(128)(4,1)}), s8[917504]{0:T(1024)(128)(4,1)S(1)}, s32[]{:S(2)}) async-start(s8[17694720]{0:T(1024)(128)(4,1)} %bitcast.83), calls=%async_computation.10 | async-start | bytes 1835008
  227.3 174.9 %all-gather.15.cloned.1.call-start = ((), (), s32[]{:S(2)}) async-start(), calls=%async_computation.7 | async-start | bytes 3981312 | tf_op jit(solution)/shard_map/all_gather | solution.py:110
  227.8 197.0 %all-gather.17.cloned.1.call-start = ((), (), s32[]{:S(2)}) async-start(), calls=%async_computation.8 | async-start | bytes 3981312 | tf_op jit(solution)/shard_map/all_gather | solution.py:111
  228.4 273.7 %all-gather.13.cloned.1.call-start = ((), (), s32[]{:S(2)}) async-start(), calls=%async_computation.6 | async-start | bytes 3981312 | tf_op jit(solution)/shard_map/all_gather | solution.py:109
  330.9 12.5 %slice-start.1 = ((s8[17694720]{0:T(1024)(128)(4,1)}), s8[4194304]{0:T(1024)(128)(4,1)S(1)}, s32[]{:S(2)}) async-start(s8[17694720]{0:T(1024)(128)(4,1)} %bitcast.83), calls=%async_computation.11 | async-start | bytes 8388608
  334.1 16.6 %copy-start.8 = (bf16[128,5120]{1,0:T(8,128)(2,1)}, bf16[128,5120]{1,0:T(8,128)(2,1)S(1)}, u32[]{:S(2)}) copy-start(bf16[128,5120]{1,0:T(8,128)(2,1)S(1)} %get-tuple-element.29) | copy-start | bytes 3932164
  361.7 34.6 %copy-start.9 = (bf16[128,5120]{1,0:T(8,128)(2,1)S(1)}, bf16[128,5120]{1,0:T(8,128)(2,1)}, u32[]{:S(2)}) copy-start(bf16[128,5120]{1,0:T(8,128)(2,1)} %copy-done.8) | copy-start | bytes 3932164
  362.9 34.6 %all-to-all-start.2 = ((bf16[128,8,640]{2,0,1:T(8,128)(2,1)}), bf16[128,8,640]{2,0,1:T(8,128)(2,1)S(1)}, u32[]{:S(2)}, u32[]{:S(2)}) async-start(bf16[128,8,640]{2,0,1:T(8,128)(2,1)} %bitcast.92), calls=%async_computation.2 | async-start | bytes 2621440 | tf_op jit(solution)/shard_map/all_to_all | solution.py:106
  367.4 159.9 %all-gather.11.cloned.1.call-start = ((), (), s32[]{:S(2)}) async-start(), calls=%async_computation.5 | async-start | bytes 3981312 | tf_op jit(solution)/shard_map/all_gather | solution.py:108
  397.4 20.1 %all-to-all-start.1 = ((bf16[128,8,640]{2,0,1:T(8,128)(2,1)}), bf16[128,8,640]{2,0,1:T(8,128)(2,1)S(1)}, u32[]{:S(2)}, u32[]{:S(2)}) async-start(bf16[128,8,640]{2,0,1:T(8,128)(2,1)} %bitcast.93), calls=%async_computation.1 | async-start | bytes 2621440 | tf_op jit(solution)/shard_map/all_to_all | solution.py:105
  417.5 28.3 %copy-start.5 = (bf16[128,8,640]{2,0,1:T(8,128)(2,1)}, bf16[128,8,640]{2,0,1:T(8,128)(2,1)S(1)}, u32[]{:S(2)}) copy-start(bf16[128,8,640]{2,0,1:T(8,128)(2,1)S(1)} %all-to-all-done.1) | copy-start | bytes 3932164
  417.5 84.6 %all-to-all-start = ((bf16[128,8,640]{2,0,1:T(8,128)(2,1)}), bf16[128,8,640]{2,0,1:T(8,128)(2,1)}, u32[]{:S(2)}, u32[]{:S(2)}) async-start(bf16[128,8,640]{2,0,1:T(8,128)(2,1)} %copy.57), calls=%async_computation | async-start | bytes 2621440 | tf_op jit(solution)/shard_map/all_to_all | solution.py:104
  479.8 15.1 %slice-start.5 = ((s8[4423680]{0:T(1024)(128)(4,1)}), s8[229376]{0:T(1024)(128)(4,1)S(1)}, s32[]{:S(2)}) async-start(s8[4423680]{0:T(1024)(128)(4,1)} %bitcast.95), calls=%async_computation.15 | async-start | bytes 458752
  (11 other events, 81.1 us)
Sparse Core Ops, SparseCore 0:
  11.2 95.8 all-gather.6
  109.6 93.3 all-gather.8
  227.4 103.5 all-reduce.2
  332.7 34.0 all-gather.14
  368.5 38.1 all-gather.16
  409.0 47.4 all-gather.12
  458.9 33.9 all-gather.10
where the time goes:
time: 573 us; the launch traced here: 565 us
  local copies, waits for them, and re-layouts  132 us (23%)
  waiting for transfers between devices  130 us (23%)
  matrix products  130 us (23%)
  other arithmetic  116 us (20%)
  blocking collectives  25.8 us (5%)
  starting transfers between devices  16.7 us (3%)
  between operations  15.3 us (3%)
    psum x1, waiting for transfers between devices, local(): lax.psum(partial_value.astype(jnp.bfloat16), 'fsdp').astype(jnp.float32)  102 us
    shift_right_arithmetic x4, local copies, waits for them, and re-layouts, signs_rows(): bits = jnp.bitwise_and(jnp.right_shift(probe[None, :, :], shifts), 1)  52.1 us
    shift_right_arithmetic x2, local copies, waits for them, and re-layouts, signs_cols(): bits = jnp.bitwise_and(jnp.right_shift(probe[:, None, :], shifts), 1)  49.2 us
    all_gather x1, waiting for transfers between devices, local(): lax.all_gather(down_master.astype(jnp.bfloat16), 'dp', axis=1, tiled=True)  26.4 us
    dot_general x3, matrix products, dot_last(): lax.dot_general(left, right, (((1,), (1,)), ((), ())), preferred_element_...  25.9 us
    psum x1, blocking collectives, local(): loss = lax.psum(0.5 * jnp.sum(diff * diff) / tokens_all, 'dp')  25.8 us
    convert_element_type x1, other arithmetic, signs_rows(): (1 - 2 * bits).reshape(32 * probe.shape[0], probe.shape[1])  23.3 us
    dot_general x1, matrix products, local(): jnp.einsum('btf,btd->bfd', actdir3, resids, preferred_element_type=jnp.fl...  21 us
  transfers between devices with their start and end apart: 10, of which 2 were waited for; matrix products, arithmetic and copies ran while one was open for 55% of the time, Pallas kernels for 0%

commit v1 on v0

v1 whole, which is shorter than its diff:
```python
import jax
import jax.numpy as jnp
from jax import lax
from jax.experimental import pallas as pl
from jax.experimental.pallas import tpu as pltpu
from jax.sharding import PartitionSpec as P

BLOCK = 16
STEP = 10


norm_eps = 1e-05
beta_one = 0.9
beta_two = 0.999
adam_eps = 1e-08


def signs_kernel(probe_ref, out_ref):
    bits = lax.shift_right_logical(probe_ref[...], pl.program_id(0)) & 1
    out_ref[...] = (1 - 2 * bits).astype(jnp.float32).astype(jnp.bfloat16)


def signs_rows(probe):
    rows, cols = probe.shape
    return pl.pallas_call(
        signs_kernel,
        grid=(32,),
        in_specs=[pl.BlockSpec((rows, cols), lambda bit: (0, 0))],
        out_specs=pl.BlockSpec((rows, cols), lambda bit: (bit, 0)),
        out_shape=jax.ShapeDtypeStruct((32 * rows, cols), jnp.bfloat16),
        cost_estimate=pl.CostEstimate(
            flops=32 * 256 * rows * cols, bytes_accessed=64 * rows * cols, transcendentals=0
        ),
    )(probe)


def dot_first(left, right):
    return lax.dot_general(
        left, right, (((0,), (0,)), ((), ())), preferred_element_type=jnp.float32
    )


def block_means(values):
    cols = values.shape[1]
    row = lax.broadcasted_iota(jnp.int32, (cols, cols), 0) // BLOCK
    col = lax.broadcasted_iota(jnp.int32, (cols, cols), 1) // BLOCK
    same = (row == col).astype(jnp.bfloat16)
    return jnp.dot(values.astype(jnp.bfloat16), same, preferred_element_type=jnp.float32) / BLOCK


def dot_last(left, right):
    return lax.dot_general(
        left, right, (((1,), (1,)), ((), ())), preferred_element_type=jnp.float32
    )


def moments(grad, hess, signs, first, second):
    diag = block_means(jnp.abs(signs * hess))
    first_new = beta_one * first + (1.0 - beta_one) * grad
    second_new = beta_two * second + (1.0 - beta_two) * diag * diag
    direction = (
        first_new
        / (1.0 - beta_one**STEP)
        / (jnp.sqrt(second_new / (1.0 - beta_two**STEP)) + adam_eps)
    )
    return (first_new, second_new, direction)


def sum_over_fsdp(value):
    parts = lax.axis_size("fsdp")
    rows, cols = value.shape
    blocks = value.reshape(parts, rows // parts, cols)
    terms = lax.all_to_all(blocks, "fsdp", split_axis=0, concat_axis=0)
    total = jnp.sum(terms.astype(jnp.float32), axis=0).astype(jnp.bfloat16)
    copies = jnp.broadcast_to(total[None], blocks.shape)
    everyone = lax.all_to_all(copies, "fsdp", split_axis=0, concat_axis=0)
    return everyone.reshape(rows, cols).astype(jnp.float32)


def local(
    tokens,
    targets,
    norm_gain,
    up_master,
    down_master,
    up_probe,
    down_probe,
    up_first,
    up_second,
    down_first,
    down_second,
):
    tok_rows = tokens.shape[0]
    tokens_all = jnp.float32(tok_rows * lax.axis_size("dp"))
    shares = lax.axis_size("dp")
    hidden = up_master.shape[1]
    own_rows = up_master.shape[0]
    values = tokens.astype(jnp.float32)
    scale = lax.rsqrt(jnp.mean(values * values, axis=-1, keepdims=True) + norm_eps)
    normed = (values * scale * norm_gain).astype(jnp.bfloat16)
    owned_in = lax.all_to_all(normed, "dp", split_axis=1, concat_axis=0, tiled=True)
    down_full = lax.all_gather(down_master.astype(jnp.bfloat16), "dp", axis=1, tiled=True)
    partial_pre = jnp.dot(
        owned_in, up_master.astype(jnp.bfloat16), preferred_element_type=jnp.float32
    ).astype(jnp.bfloat16)
    pieces = lax.all_to_all(
        partial_pre.reshape(shares, tok_rows, hidden), "dp", split_axis=0, concat_axis=0
    )
    up_signs = signs_rows(up_probe)
    down_signs_t = signs_rows(down_probe.T)
    preact_dir = jnp.dot(normed, up_signs, preferred_element_type=jnp.float32)
    preact = jnp.sum(pieces.astype(jnp.float32), axis=0)
    logistic = jax.nn.sigmoid(preact)
    active = (preact * logistic).astype(jnp.bfloat16)
    slopes = logistic * (1.0 + preact * (1.0 - logistic))
    curves = logistic * (1.0 - logistic) * (2.0 + preact * (1.0 - 2.0 * logistic))
    active_dir = (slopes * preact_dir).astype(jnp.bfloat16)
    partial_value = jnp.dot(active, down_full, preferred_element_type=jnp.float32)
    partial_dir = jnp.dot(active_dir, down_full, preferred_element_type=jnp.float32) + dot_last(
        active, down_signs_t
    )
    hidden_forward = lax.all_gather(jnp.stack([active, active_dir]), "dp", axis=0)
    output = sum_over_fsdp(partial_value.astype(jnp.bfloat16))
    output_dir = sum_over_fsdp(partial_dir.astype(jnp.bfloat16))
    diff = output - targets.astype(jnp.float32)
    residual = (diff / tokens_all).astype(jnp.bfloat16)
    residual_dir = (output_dir / tokens_all).astype(jnp.bfloat16)
    loss = lax.psum(0.5 * jnp.sum(diff * diff) / tokens_all, "dp")
    grad_active = dot_last(residual, down_full)
    hess_active = dot_last(residual_dir, down_full) + jnp.dot(
        residual, down_signs_t, preferred_element_type=jnp.float32
    )
    grad_preact = (slopes * grad_active).astype(jnp.bfloat16)
    hess_preact = (curves * preact_dir * grad_active + slopes * hess_active).astype(jnp.bfloat16)
    hidden_backward = lax.all_gather(jnp.stack([grad_preact, hess_preact]), "dp", axis=0)
    owned_res = lax.all_to_all(residual, "dp", split_axis=1, concat_axis=0, tiled=True)
    owned_dir = lax.all_to_all(residual_dir, "dp", split_axis=1, concat_axis=0, tiled=True)
    act_all = hidden_forward[:, 0].reshape(shares * tok_rows, hidden)
    actdir_all = hidden_forward[:, 1].reshape(shares * tok_rows, hidden)
    grad_all = hidden_backward[:, 0].reshape(shares * tok_rows, hidden)
    hess_all = hidden_backward[:, 1].reshape(shares * tok_rows, hidden)
    down_grad = dot_first(act_all, owned_res)
    down_hess = dot_first(act_all, owned_dir) + dot_first(actdir_all, owned_res)
    up_grad = dot_first(owned_in, grad_all)
    up_hess = dot_first(owned_in, hess_all)
    offset = lax.axis_index("dp") * own_rows
    up_own = lax.dynamic_slice_in_dim(up_signs, offset, own_rows, 0).astype(jnp.float32)
    down_own = lax.dynamic_slice_in_dim(down_signs_t, offset, own_rows, 0).T.astype(jnp.float32)
    up_moment, up_curvature, up_step = moments(up_grad, up_hess, up_own, up_first, up_second)
    down_moment, down_curvature, down_step = moments(
        down_grad, down_hess, down_own, down_first, down_second
    )
    return (loss, up_moment, up_curvature, up_step, down_moment, down_curvature, down_step)


def solution(mesh):
    placed = (
        P("dp", None),
        P("dp", None),
        P(),
        P("dp", "fsdp"),
        P("fsdp", "dp"),
        P(None, "fsdp"),
        P("fsdp", None),
        P("dp", "fsdp"),
        P("dp", "fsdp"),
        P("fsdp", "dp"),
        P("fsdp", "dp"),
    )
    return jax.shard_map(
        local,
        mesh=mesh,
        in_specs=placed,
        out_specs=(
            P(),
            P("dp", "fsdp"),
            P("dp", "fsdp"),
            P("dp", "fsdp"),
            P("fsdp", "dp"),
            P("fsdp", "dp"),
            P("fsdp", "dp"),
        ),
        check_vma=False,
    )
```

time: 573 us -> 540 us (0.942)
  blocking collectives: 25.8 us -> 246 us
  waiting for transfers between devices: 130 us -> 17.4 us
  other arithmetic: 116 us -> 18.5 us
  local copies, waits for them, and re-layouts: 132 us -> 58.8 us
  Pallas kernels: 0 us -> 36.1 us
  matrix products: 130 us -> 124 us
    all_to_all x0 -> x5, blocking collectives: none -> 215 us  [the longest x1 78.2 us: local(): lax.all_to_all(partial_pre.reshape(shares, tok_rows, hidden), 'dp', split...]
    psum x1 -> x0, waiting for transfers between devices: 102 us -> none  [local(): lax.psum(partial_value.astype(jnp.bfloat16), 'fsdp').astype(jnp.float32)]
    shift_right_arithmetic x6 -> x0, local copies, waits for them, and re-layouts: 101 us -> none  [the longest x4 52.1 us: signs_rows(): bits = jnp.bitwise_and(jnp.right_shift(probe[None, :, :], shifts), 1)]
    reduce_sum x6 -> x3, other arithmetic: 40.5 us -> 2.49 us  [the longest x2 1.98 us: sum_over_fsdp(): total = jnp.sum(terms.astype(jnp.float32), axis=0).astype(jnp.bfloat16)]
    convert_element_type x3 -> x1, other arithmetic: 37.6 us -> 1.04 us  [local(): active = (preact * logistic).astype(jnp.bfloat16)]
    pallas_call x0 -> x2, Pallas kernels: none -> 36.1 us  [signs_rows(): pl.pallas_call(signs_kernel, grid=(32,), in_specs=[pl.BlockSpec((rows, co...]
    unnamed x51 -> x42, local copies, waits for them, and re-layouts: 11.4 us -> 42.1 us
    dot_general x7 -> x8, matrix products: 85.8 us -> 62.4 us  [the longest x2 28.3 us: block_means(): jnp.dot(values.astype(jnp.bfloat16), same, preferred_element_type=jnp.flo...]
  transfers between devices with their start and end apart: 10 -> 6, of which waited for: 2 -> 2; matrix products, arithmetic and copies ran while one was open for 55% -> 24% of each run, Pallas kernels for 0% -> 7%
where the time goes in v1:
time: 540 us; the launch traced here: 532 us
  blocking collectives  246 us (46%)
  matrix products  124 us (23%)
  local copies, waits for them, and re-layouts  58.8 us (11%)
  Pallas kernels  36.1 us (7%)
  other arithmetic  18.5 us (3%)
  waiting for transfers between devices  17.4 us (3%)
  starting transfers between devices  16.2 us (3%)
  between operations  15.3 us (3%)
    all_to_all x1, blocking collectives, local(): lax.all_to_all(partial_pre.reshape(shares, tok_rows, hidden), 'dp', split...  78.2 us
    all_to_all x2, blocking collectives, sum_over_fsdp(): terms = lax.all_to_all(blocks, 'fsdp', split_axis=0, concat_axis=0)  70.4 us
    unnamed x42, local copies, waits for them, and re-layouts  42.1 us
    pallas_call x2, Pallas kernels, signs_rows(): pl.pallas_call(signs_kernel, grid=(32,), in_specs=[pl.BlockSpec((rows, co...  36.1 us
    all_to_all x1, blocking collectives, sum_over_fsdp(): everyone = lax.all_to_all(copies, 'fsdp', split_axis=0, concat_axis=0)  33.7 us
    all_to_all x1, blocking collectives, local(): lax.all_to_all(normed, 'dp', split_axis=1, concat_axis=0, tiled=True)  32.3 us
    dot_general x3, matrix products, dot_last(): lax.dot_general(left, right, (((1,), (1,)), ((), ())), preferred_element_...  31.4 us
    psum x1, blocking collectives, local(): loss = lax.psum(0.5 * jnp.sum(diff * diff) / tokens_all, 'dp')  31.2 us
  transfers between devices with their start and end apart: 6, of which 2 were waited for; matrix products, arithmetic and copies ran while one was open for 24% of the time, Pallas kernels for 7%

profile of v1, /device:TPU:1, one launch (start us, length us, event | category | flops | bytes accessed | tf_op | source)
XLA Modules:
  0.0 531.8 jit_solution(13517988522932569952)
XLA Ops:
  14.9 32.3 %all_to_all.79 = bf16[128,8,640]{0,2,1:T(8,128)(2,1)S(1)} all-to-all(bf16[128,8,640]{0,2,1:T(8,128)(2,1)S(1)} %bitcast.125), channel_id=1, replica_groups=mesh['dp'=8,'fsdp'=4] {'dp'}, dimensions={1} | all-to-all | bytes 2621440 | tf_op jit(solution)/shard_map/all_to_all | solution.py:101
  48.6 5.6 %fusion.32 = bf16[216,8,8,128]{3,2,1,0:T(8,128)(2,1)S(1)} fusion(bf16[1024,640]{1,0:T(8,128)(2,1)} %bitcast.139, f32[640,1728]{0,1:T(8,128)} %param.14), kind=kOutput, calls=%fused_computation.51 | convolution fusion | flops 2267799552 | bytes 9273344 | tf_op jit(solution)/shard_map/dot_general | solution.py:103
  54.8 78.2 %all_to_all.80 = bf16[8,128,1728]{1,2,0:T(8,128)(2,1)S(1)} all-to-all(bf16[8,128,1728]{1,2,0:T(8,128)(2,1)S(1)} %bitcast.124), channel_id=1, replica_groups=mesh['dp'=8,'fsdp'=4] {'dp'}, dimensions={0} | all-to-all | bytes 7077888 | tf_op jit(solution)/shard_map/all_to_all | solution.py:106
  133.6 17.0 %all-gather.6.cloned.1.call-done = bf16[1728,5120]{1,0:T(8,128)(2,1)} async-done(((bf16[1728,640]{1,0:T(8,128)(2,1)}), bf16[1728,5120]{1,0:T(8,128)(2,1)}) %all-gather.6.cloned.1.call-update) | async-done | bytes 17694736 | tf_op jit(solution)/shard_map/all_gather | solution.py:102
  150.6 8.7 %convolution_convert_fusion = bf16[128,5120]{1,0:T(8,128)(2,1)S(1)} fusion(bf16[1728,5120]{1,0:T(8,128)(2,1)} %all-gather.6.cloned.1.call-done, f32[128,1728]{0,1:T(8,128)S(1)} %convert_reduce_fusion), kind=kOutput, calls=%fused_computation.10 | convolution fusion | flops 2266685440 | bytes 19890176 | tf_op jit(solution)/shard_map/dot_general | solution.py:118
  159.2 35.6 %all_to_all.81 = bf16[4,32,5120]{2,1,0:T(8,128)(2,1)S(1)} all-to-all(bf16[4,32,5120]{2,1,0:T(8,128)(2,1)S(1)} %bitcast.128), channel_id=1, replica_groups=mesh['dp'=8,'fsdp'=4] {'fsdp'}, dimensions={0} | all-to-all | bytes 2621440 | tf_op jit(solution)/shard_map/all_to_all | solution.py:73
  202.8 18.1 %shard_map.162 = bf16[5120,1728]{1,0:T(8,128)(2,1)} custom-call(s32[160,1728]{1,0:T(8,128)} %probe_ref.1), custom_call_target="tpu_custom_call" | custom-call | flops 2264924160 | bytes 17694720 | tf_op jit(solution)/shard_map/pallas_call | solution.py:25
  220.9 11.0 %fusion.70 = f32[128,1728]{0,1:T(8,128)S(1)} fusion(bf16[128,5120]{0,1:T(8,128)(2,1)S(1)} %fusion.26, bf16[5120,1728]{1,0:T(8,128)(2,1)} %shard_map.162), kind=kOutput, calls=%fused_computation.99 | convolution fusion | flops 2264924160 | bytes 19890176 | tf_op jit(solution)/shard_map/dot_general | solution.py:111
  236.2 8.5 %fusion.69 = f32[128,1728]{0,1:T(8,128)S(1)} fusion(bf16[128,5120]{1,0:T(8,128)(2,1)S(1)} %get-tuple-element.11, bf16[1728,5120]{1,0:T(8,128)(2,1)} %all-gather.6.cloned.1.call-done), kind=kOutput, calls=%fused_computation.98 | convolution fusion | flops 2264924160 | bytes 19890176 | tf_op jit(solution)/shard_map/dot_general | solution.py:52
  247.3 18.0 %shard_map.163 = bf16[5120,1728]{1,0:T(8,128)(2,1)} custom-call(s32[160,1728]{1,0:T(8,128)} %bitcast.145), custom_call_target="tpu_custom_call" | custom-call | flops 2264924160 | bytes 17694720 | tf_op jit(solution)/shard_map/pallas_call | solution.py:25
  265.4 10.2 %fusion.71 = f32[128,5120]{1,0:T(8,128)} fusion(bf16[128,1728]{0,1:T(8,128)(2,1)S(1)} %get-tuple-element.14, bf16[1728,5120]{1,0:T(8,128)(2,1)} %all-gather.6.cloned.1.call-done), kind=kOutput, calls=%fused_computation.100 | convolution fusion | flops 2264924160 | bytes 20758528 | tf_op jit(solution)/shard_map/dot_general | solution.py:119
  275.6 14.3 %fusion.7 = bf16[128,5120]{1,0:T(8,128)(2,1)} fusion(f32[128,5120]{1,0:T(8,128)} %fusion.71, bf16[5120,1728]{1,0:T(8,128)(2,1)} %shard_map.163, f32[128,1728]{0,1:T(8,128)S(1)} %convert_reduce_fusion), kind=kOutput, calls=%fused_computation.11 | convolution fusion | flops 2267340800 | bytes 22511616 | tf_op jit(solution)/shard_map/dot_general | solution.py:52
  289.9 34.9 %all_to_all.82 = bf16[4,32,5120]{2,1,0:T(8,128)(2,1)S(1)} all-to-all(bf16[4,32,5120]{2,1,0:T(8,128)(2,1)} %bitcast.144), channel_id=1, replica_groups=mesh['dp'=8,'fsdp'=4] {'fsdp'}, dimensions={0} | all-to-all | bytes 2621440 | tf_op jit(solution)/shard_map/all_to_all | solution.py:73
  326.8 33.7 %all_to_all.83 = bf16[4,32,5120]{2,1,0:T(8,128)(2,1)S(1)} all-to-all(bf16[4,32,5120]{2,1,0:T(8,128)(2,1)S(1)} %broadcast_in_dim.5), channel_id=1, replica_groups=mesh['dp'=8,'fsdp'=4] {'fsdp'}, dimensions={0} | all-to-all | bytes 2621440 | tf_op jit(solution)/shard_map/all_to_all | solution.py:76
  360.8 8.6 %fusion.72 = f32[128,1728]{0,1:T(8,128)S(1)} fusion(bf16[128,5120]{1,0:T(8,128)(2,1)S(1)} %bitcast.122, bf16[1728,5120]{1,0:T(8,128)(2,1)} %all-gather.6.cloned.1.call-done), kind=kOutput, calls=%fused_computation.101 | convolution fusion | flops 2264924160 | bytes 19890176 | tf_op jit(solution)/shard_map/dot_general | solution.py:52
  369.5 11.7 %fusion.30 = bf16[1,128,1728]{1,2,0:T(8,128)(2,1)S(1)} fusion(f32[128,1728]{0,1:T(8,128)S(1)} %fusion.72, bf16[128,5120]{1,0:T(8,128)(2,1)S(1)} %get-tuple-element.11, bf16[5120,1728]{1,0:T(8,128)(2,1)} %shard_map.163, f32[128,1728]{0,1:T(8,128)S(1)} %copy-done.3, f32[128,1728]{0,1:T(8,128)S(1)} %copy-done.1, f32[128,1728]{0,1:T(8,128)S(1)} %convert_reduce_fusion), kind=kOutput, calls=%fused_computation.49 | convolution fusion | flops 2269126656 | bytes 22986752 | tf_op jit(solution)/shard_map/dot_general | solution.py:130
  391.4 31.2 %psum.7 = f32[]{:T(128)} all-reduce(f32[]{:T(128)S(6)} %div.96), channel_id=1, replica_groups=mesh['dp'=8,'fsdp'=4] {'dp'}, use_global_device_ids=true, to_apply=%region_4.0 | all-reduce | flops 1 | bytes 8 | tf_op jit(solution)/shard_map/psum | solution.py:128
  425.5 5.7 %all-to-all-start.7 = ((bf16[128,8,640]{2,0,1:T(8,128)(2,1)}), bf16[128,8,640]{2,0,1:T(8,128)(2,1)}, u32[]{:S(2)}, u32[]{:S(2)}) async-start(bf16[128,8,640]{2,0,1:T(8,128)(2,1)} %copy.55), calls=%async_computation.7 | async-start | bytes 2621440 | tf_op jit(solution)/shard_map/all_to_all | solution.py:137
  434.9 10.1 %copy.64 = bf16[8,1,128,1728]{2,0,3,1:T(8,128)(2,1)S(1)} copy(bf16[8,1,128,1728]{2,3,1,0:T(8,128)(2,1)S(1)} %get-tuple-element.8) | data formatting | bytes 7077888
  445.0 10.2 %copy.65 = bf16[8,1,128,1728]{2,0,3,1:T(8,128)(2,1)S(1)} copy(bf16[8,1,128,1728]{2,3,1,0:T(8,128)(2,1)S(1)} %get-tuple-element.7) | data formatting | bytes 7077888
  464.6 16.5 %add_divide_fusion = (f32[1728,640]{1,0:T(8,128)}, f32[1728,640]{1,0:T(8,128)}) fusion(f32[1728,640]{1,0:T(8,128)} %multiply_add_fusion.1, s32[640]{0:T(1024)} %get-tuple-element.21, s32[640]{0:T(1024)} %get-tuple-element.22, pred[640]{0:T(1024)(128)(4,1)} %fusion.59, f32[1728,640]{0,1:T(8,128)} %fusion.10, bf16[1024,640]{1,0:T(8,128)(2,1)} %bitcast.19, ...), kind=kOutput, calls=%fused_computation.16 | convolution fusion | flops 3697213440 | bytes 29444100 | tf_op jit(solution)/shard_map/dot_general | solution.py:48
  484.7 10.3 %copy.62 = bf16[8,1,128,1728]{2,0,3,1:T(8,128)(2,1)S(1)} copy(bf16[8,1,128,1728]{2,3,1,0:T(8,128)(2,1)S(1)} %get-tuple-element.10) | data formatting | bytes 7077888
  495.0 10.3 %copy.63 = bf16[8,1,128,1728]{2,0,3,1:T(8,128)(2,1)S(1)} copy(bf16[8,1,128,1728]{2,3,1,0:T(8,128)(2,1)S(1)} %get-tuple-element.9) | data formatting | bytes 7077888
  513.0 11.8 %add_divide_fusion.1 = (f32[640,1728]{0,1:T(8,128)}, f32[640,1728]{0,1:T(8,128)}) fusion(f32[640,1728]{0,1:T(8,128)S(1)} %multiply_add_fusion.3, s32[1728]{0:T(1024)S(1)} %get-tuple-element.19, s32[1728]{0:T(1024)S(1)} %get-tuple-element.20, pred[1728]{0:T(1024)(128)(4,1)S(1)} %copy-done.10, f32[640,1728]{0,1:T(8,128)S(1)} %bitcast.151, ...), kind=kOutput, calls=%fused_computation.19 | convolution fusion | flops 3840970752 | bytes 19922112 | tf_op jit(solution)/shard_map/dot_general | solution.py:48
  (84 shorter events, 64.1 us)
Async XLA Ops:
  7.2 4.0 copy-start.6
  7.2 143.4 %all-gather.6.cloned.1.call-start = ((), (), s32[]{:S(2)}) async-start(), calls=%async_computation.8 | async-start | bytes 19906560 | tf_op jit(solution)/shard_map/all_gather | solution.py:102
  11.2 1.5 copy-start.9
  198.0 35.3 %all-to-all-start.3 = ((bf16[4,32,5120]{2,1,0:T(8,128)(2,1)}), bf16[4,32,5120]{2,1,0:T(8,128)(2,1)}, u32[]{:S(2)}, u32[]{:S(2)}) async-start(bf16[4,32,5120]{2,1,0:T(8,128)(2,1)} %broadcast_in_dim.4), calls=%async_computation.3 | async-start | bytes 2621440 | tf_op jit(solution)/shard_map/all_to_all | solution.py:76
  202.3 229.0 %all-gather.10.cloned.1.call-start = ((), (), s32[]{:S(2)}) async-start(), calls=%async_computation.10 | async-start | bytes 7962624 | tf_op jit(solution)/shard_map/all_gather | solution.py:122
  231.9 12.9 %copy-start = (f32[128,1728]{0,1:T(8,128)}, f32[128,1728]{0,1:T(8,128)S(1)}, u32[]{:S(2)}) copy-start(f32[128,1728]{0,1:T(8,128)S(1)} %fusion.70) | copy-start | bytes 2654212
  244.8 1.2 copy-start.2
  244.8 1.3 copy-start.5
  247.1 234.0 %all-gather.8.cloned.1.call-start = ((), (), s32[]{:S(2)}) async-start(), calls=%async_computation.9 | async-start | bytes 7962624 | tf_op jit(solution)/shard_map/all_gather | solution.py:135
  360.8 8.7 %copy-start.1 = (f32[128,1728]{0,1:T(8,128)S(1)}, f32[128,1728]{0,1:T(8,128)}, u32[]{:S(2)}) copy-start(f32[128,1728]{0,1:T(8,128)} %copy-done) | copy-start | bytes 2654212
  360.8 8.7 %copy-start.3 = (f32[128,1728]{0,1:T(8,128)S(1)}, f32[128,1728]{0,1:T(8,128)}, u32[]{:S(2)}) copy-start(f32[128,1728]{0,1:T(8,128)} %copy-done.2) | copy-start | bytes 2654212
  369.5 11.7 %copy-start.4 = (bf16[1,128,1728]{1,2,0:T(8,128)(2,1)S(1)}, bf16[1,128,1728]{1,2,0:T(8,128)(2,1)}, u32[]{:S(2)}) copy-start(bf16[1,128,1728]{1,2,0:T(8,128)(2,1)} %get-tuple-element.13) | copy-start | bytes 1327108
  383.6 39.1 %all-to-all-start.6 = ((bf16[128,8,640]{0,2,1:T(8,128)(2,1)}), bf16[128,8,640]{0,2,1:T(8,128)(2,1)S(1)}, u32[]{:S(2)}, u32[]{:S(2)}) async-start(bf16[128,8,640]{0,2,1:T(8,128)(2,1)} %bitcast.130), calls=%async_computation.6 | async-start | bytes 2621440 | tf_op jit(solution)/shard_map/all_to_all | solution.py:136
  425.5 39.0 %all-to-all-start.7 = ((bf16[128,8,640]{2,0,1:T(8,128)(2,1)}), bf16[128,8,640]{2,0,1:T(8,128)(2,1)}, u32[]{:S(2)}, u32[]{:S(2)}) async-start(bf16[128,8,640]{2,0,1:T(8,128)(2,1)} %copy.55), calls=%async_computation.7 | async-start | bytes 2621440 | tf_op jit(solution)/shard_map/all_to_all | solution.py:137
  445.0 10.3 %copy-start.8 = (bf16[8,128,640]{2,1,0:T(8,128)(2,1)S(1)}, bf16[8,128,640]{2,1,0:T(8,128)(2,1)}, u32[]{:S(2)}) copy-start(bf16[8,128,640]{2,1,0:T(8,128)(2,1)} %copy.54) | copy-start | bytes 3932164
  445.0 15.1 %slice-start = ((s8[4423680]{0:T(1024)(128)(4,1)}), s8[4194304]{0:T(1024)(128)(4,1)S(1)}, s32[]{:S(2)}) async-start(s8[4423680]{0:T(1024)(128)(4,1)} %bitcast.146), calls=%async_computation.11 | async-start | bytes 8388608
  455.3 4.8 slice-start.1
  495.0 10.4 %copy-start.7 = (bf16[8,128,640]{2,1,0:T(8,128)(2,1)S(1)}, bf16[8,128,640]{2,1,0:T(8,128)(2,1)}, u32[]{:S(2)}) copy-start(bf16[8,128,640]{2,1,0:T(8,128)(2,1)} %copy.47) | copy-start | bytes 3932164
  495.0 14.8 %slice-start.2 = ((s8[4423680]{0:T(1024)(128)(4,1)}), s8[4194304]{0:T(1024)(128)(4,1)S(1)}, s32[]{:S(2)}) async-start(s8[4423680]{0:T(1024)(128)(4,1)} %bitcast.148), calls=%async_computation.13 | async-start | bytes 8388608
  505.3 4.5 slice-start.3
  505.3 7.7 %slice-start.4 = ((s8[4423680]{0:T(1024)(128)(4,1)}), s8[4194304]{0:T(1024)(128)(4,1)S(1)}, s32[]{:S(2)}) async-start(s8[4423680]{0:T(1024)(128)(4,1)} %bitcast.150), calls=%async_computation.15 | async-start | bytes 8388608
  509.8 3.2 copy-start.10
  509.9 3.2 slice-start.5
  513.0 11.9 %copy-start.11 = (f32[640,1728]{0,1:T(8,128)}, f32[640,1728]{0,1:T(8,128)S(1)}, u32[]{:S(2)}) copy-start(f32[640,1728]{0,1:T(8,128)S(1)} %multiply_add_fusion.3) | copy-start | bytes 13271044
Sparse Core Ops, SparseCore 0:
  11.3 139.2 all-gather.5
  247.2 49.9 all-gather.9
  382.3 69.3 all-gather.7
